TPU v7x, 32 devices: a whole 2x2x4 slice. The times are simulated.
32 devices in a mesh: cuts: 2 (over x), mode: 16 (over z, y, core).
Axes of the slice: x: 2, y: 2, z: 4, core: 2. Of those that a mesh axis runs over, the one named last changes fastest.
Arguments:
- stem_tensor: float32 [2, 2, 16, 512, 512], P(None, 'cuts', 'mode'), parts along dimension 1, may hold values from -6 to 6
- branch_tensors: float32 [4, 2, 512, 512], replicated, may hold values from -0.1875 to 0.1875
- branch_order: int32 [4], replicated, may hold values from 0 to 3, each once
Outputs:
- new_stem: float32 [2, 2, 16, 512, 512], P(None, 'cuts', 'mode'), parts along dimension 1
There are 2 independent parts, one for each index of `cuts`. A program takes and returns all parts, laid end to end along the dimension named above; an argument that names none is the same for every part. Nothing has to cross between parts.
Inputs may be any that keep to these rules, and one draw needn't show every extreme that they name: `branch_order`: a permutation of the 4 branch tensors.
All inputs are finite; a program needn't handle non-finite values.
Results may differ from a plain program's by a relative error of at most 0.00007.
Values sent between devices are 32-bit elements; how exact they have to be, the bound alone decides.
A program may use at most 64 MiB of HBM per device.

v0:
```python
import functools

import jax
import jax.numpy as jnp
from jax import lax
from jax.experimental import pallas as pl
from jax.experimental.pallas import tpu as pltpu
from jax.sharding import PartitionSpec as P

MESH = pl.DeviceIdType.MESH
LANES = 128
F32, BF16 = jnp.float32, jnp.bfloat16


def flip(value, mask, size):
    result, bit = 0, 1
    while bit < size:
        digit = lax.rem(lax.div(value, bit), 2)
        result = result + (1 - digit if (mask // bit) % 2 else digit) * bit
        bit *= 2
    return result


def split(value):
    high = value.astype(BF16)
    return high, (value - high.astype(F32)).astype(BF16)


def dot(a, b):
    return jnp.dot(a, b, preferred_element_type=F32)


def dot3(high, low, right_high, right_low):
    return dot(high, right_high) + (dot(high, right_low) + dot(low, right_high))


def complex_rows(rows, right_high, right_low):
    m = rows.shape[0] // 2
    high, low = split(rows)
    by_real = dot3(high, low, right_high[0], right_low[0])
    by_imag = dot3(high, low, right_high[1], right_low[1])
    return by_real[:m] - by_imag[m:], by_imag[:m] + by_real[m:]


def kernel(n, order_ref, stem_ref, branch_ref, out_ref, stem, xh, xl, bh, bl, dh, dl, wh, wl,
           lch, lcl, lct, sent, got, acc, load_sem, branch_sem, out_sem, send_sem, recv_sem, *branch):
    bw = stem.shape[1]
    rows = bw // n
    per = LANES // rows
    groups = n // per
    me = lax.axis_index("mode")
    z, q = lax.div(me, per), lax.rem(me, per)
    sequence = [groups // 2] + [s for s in range(1, groups) if s != groups // 2] + [0]
    early = sequence[: groups // 2]

    def column(s):
        return pl.ds(pl.multiple_of(flip(z, s, groups) * LANES, LANES), LANES)

    stem_copies = [pltpu.make_async_copy(stem_ref.at[part], stem.at[part], load_sem.at[part]) for part in range(2)]
    branch_copies = {}
    for s in sequence:
        branch_copies[s] = pltpu.make_async_copy(branch_ref.at[:, :, :, column(s)], branch[s], branch_sem.at[s])
        if s == sequence[0]:
            branch_copies[s].start()
    for copy in stem_copies:
        copy.start()

    barrier = pltpu.get_barrier_semaphore()
    for k in range(1, n):
        pl.semaphore_signal(barrier, inc=1, device_id={"mode": flip(me, k, n)}, device_id_type=MESH)
    o0, o1, o2, o3 = (order_ref[k] for k in range(4))

    def left_rows(s):
        return jnp.concatenate([branch[s][o0, part].T for part in range(2)], axis=0)

    def first_rows(s):
        return complex_rows(left_rows(s), xh, xl)

    def hop(s, k):
        j = flip(q, k, per)
        return pltpu.make_async_remote_copy(
            src_ref=sent.at[s, j], dst_ref=got.at[s, q], send_sem=send_sem.at[s, k], recv_sem=recv_sem.at[s, q],
            device_id={"mode": flip(z, s, groups) * per + j}, device_id_type=MESH)

    def own(s):
        return pltpu.make_async_copy(sent.at[s, q], got.at[s, q], recv_sem.at[s, q])

    def send(s, real, imag):
        for j in range(per):
            sent[s, j, 0] = real[j * rows:(j + 1) * rows]
            sent[s, j, 1] = imag[j * rows:(j + 1) * rows]
        for k in range(per):
            own(s).start() if s == 0 and k == 0 else hop(s, k).start()

    branch_copies[sequence[0]].wait()
    high, low = split(left_rows(sequence[0]))
    by = []
    for part in range(2):
        stem_copies[part].wait()
        if part == 1:
            for s in sequence[1:]:
                branch_copies[s].start()
        xh[part], xl[part] = split(stem[part])
        by.append(dot3(high, low, xh[part], xl[part]))
    real, imag = by[0][:LANES] - by[1][LANES:], by[1][:LANES] + by[0][LANES:]
    pl.semaphore_wait(barrier, n - 1)
    send(sequence[0], real, imag)
    for s in early[1:]:
        branch_copies[s].wait()
        send(s, *first_rows(s))
    for s in sequence[len(early):]:
        branch_copies[s].wait()

    for s in range(groups):
        for part in range(2):
            bh[part, :, column(s)], bl[part, :, column(s)] = split(branch[s][o1, part])
            dh[part, :, column(s)], dl[part, :, column(s)] = split(branch[s][o3, part])

    def both(i, carry):
        at = pl.ds(pl.multiple_of(i * LANES, LANES), LANES)
        high = jnp.concatenate([bh[0, at], bh[1, at]], axis=0)
        low = jnp.concatenate([bl[0, at], bl[1, at]], axis=0)
        by_real = dot3(high, low, dh[0], dl[0])
        by_imag = dot3(high, low, dh[1], dl[1])
        wh[0, at], wl[0, at] = split(by_real[:LANES] - by_imag[LANES:])
        wh[1, at], wl[1, at] = split(by_imag[:LANES] + by_real[LANES:])
        return carry

    lax.fori_loop(0, bw // LANES, both, 0)

    for s in sequence[len(early):]:
        real, imag = first_rows(s)
        send(s, *complex_rows(jnp.concatenate([real, imag], axis=0), wh, wl))

    last = sequence[-2]

    def third_rows(t, part, s):
        if s != last:
            return branch[t][o2, part, column(s), :]
        base = flip(z, s, groups) * LANES
        return jnp.concatenate([
            branch[t][o2, part, pl.ds(pl.multiple_of(base + flip(q, k, per) * rows, rows), rows), :]
            for k in range(per)], axis=0)

    for s in range(groups):
        for t in range(groups):
            real, imag = (split(third_rows(t, part, s).T) for part in range(2))
            top = column(t)
            low_half = pl.ds(pl.multiple_of(bw + flip(z, t, groups) * LANES, LANES), LANES)
            for ref, r, i in ((lch, real[0], imag[0]), (lcl, real[1], imag[1])):
                ref[s, top, :LANES] = r
                ref[s, top, LANES:] = -i
                ref[s, low_half, :LANES] = i
                ref[s, low_half, LANES:] = r
            if s == last:
                tail = slice(LANES - rows, LANES)
                for place, (r, i) in enumerate(((real[0], imag[0]), (real[0], imag[0]), (real[1], imag[1]))):
                    at = slice(2 * place * rows, (2 * place + 1) * rows)
                    after = slice((2 * place + 1) * rows, (2 * place + 2) * rows)
                    lct[top, at] = r[:, tail]
                    lct[top, after] = -i[:, tail]
                    lct[low_half, at] = i[:, tail]
                    lct[low_half, after] = r[:, tail]

    arrivals = [0] + [s for s in early if s != groups // 2] + [groups // 2] + [s for s in sequence[len(early):] if s]
    tile = 2 * LANES

    def arrive(s, j):
        pltpu.make_async_copy(got.at[s, j], got.at[s, j], recv_sem.at[s, j]).wait()

    for index, s in enumerate(arrivals):
        places = [flip(q, k, per) if s == last else k for k in range(per)]
        if s == last:
            final = places.pop()
        for j in places:
            arrive(s, j)
        blank = [jnp.zeros((rows, bw), F32)] * (per - len(places))
        arrived = jnp.concatenate([piece for part in range(2) for piece in [got[s, j, part] for j in places] + blank], axis=0)
        if s in early:
            arrived = jnp.concatenate(complex_rows(arrived, wh, wl), axis=0)
        right_high, right_low = split(arrived)
        for i in range(2 * bw // tile):
            at = slice(i * tile, (i + 1) * tile)
            add = dot3(lch[s, at], lcl[s, at], right_high, right_low)
            acc[at] = add if index == 0 else acc[at] + add
    arrive(last, final)
    high, low = split(jnp.concatenate([got[last, final, 0], got[last, final, 1]], axis=0))
    right = jnp.concatenate([high, low, high], axis=0)
    for i in range(2 * bw // tile):
        at = slice(i * tile, (i + 1) * tile)
        acc[at] = acc[at] + dot(lct[at, : 6 * rows], right)
        part, row = divmod(i * tile, bw)
        pltpu.make_async_copy(acc.at[at], out_ref.at[part, pl.ds(row, tile)], out_sem.at[i]).start()
    for i in range(2 * bw // tile):
        part, row = divmod(i * tile, bw)
        pltpu.make_async_copy(acc.at[pl.ds(i * tile, tile)], out_ref.at[part, pl.ds(row, tile)], out_sem.at[i]).wait()
    for s in range(groups):
        for k in range(per):
            if s or k:
                hop(s, k).wait_send()


def fused(n, stem_tensor, branch_tensors, branch_order):
    bw = stem_tensor.shape[-1]
    rows = bw // n
    per = LANES // rows
    groups = n // per
    square = pltpu.VMEM((2, bw, bw), BF16)
    hbm = functools.partial(pltpu.with_memory_space_constraint, memory_space=pltpu.HBM)
    window = pltpu.VMEM((groups, 2 * bw, 2 * LANES), BF16)
    return pl.pallas_call(
        functools.partial(kernel, n),
        out_shape=jax.ShapeDtypeStruct((2, bw, bw), F32),
        in_specs=[pl.BlockSpec(memory_space=pltpu.SMEM)] + [pl.BlockSpec(memory_space=pl.ANY)] * 2,
        out_specs=pl.BlockSpec(memory_space=pl.ANY),
        scratch_shapes=[
            pltpu.VMEM((2, bw, bw), F32),
            *[square] * 8,
            window,
            window,
            pltpu.VMEM((2 * bw, 2 * LANES), BF16),
            pltpu.VMEM((groups, per, 2, rows, bw), F32),
            pltpu.VMEM((groups, per, 2, rows, bw), F32),
            pltpu.VMEM((2 * bw, bw), F32),
            pltpu.SemaphoreType.DMA((2,)),
            pltpu.SemaphoreType.DMA((groups,)),
            pltpu.SemaphoreType.DMA((bw // LANES,)),
            pltpu.SemaphoreType.DMA((groups, per)),
            pltpu.SemaphoreType.DMA((groups, per)),
            *[pltpu.VMEM((4, 2, bw, LANES), F32)] * groups,
        ],
        compiler_params=pltpu.CompilerParams(collective_id=0, has_side_effects=True, vmem_limit_bytes=32 << 20),
    )(hbm(branch_order), hbm(stem_tensor.reshape(2, bw, bw)), hbm(branch_tensors)).reshape(stem_tensor.shape)


def complex_product(first, second, form):
    high = lax.Precision.HIGHEST
    real = jnp.einsum(form, first[0], second[0], precision=high) - jnp.einsum(form, first[1], second[1], precision=high)
    imag = jnp.einsum(form, first[0], second[1], precision=high) + jnp.einsum(form, first[1], second[0], precision=high)
    return jnp.stack([real, imag])


def plain(stem_tensor, branch_tensors, branch_order):
    field = stem_tensor[:, :, 0]
    chosen = [branch_tensors[branch_order[index]] for index in range(4)]
    field = complex_product(field, chosen[0], "sce,cd->sde")
    field = complex_product(field, chosen[1], "sce,ed->scd")
    moved = lax.all_to_all(field[:, :, None], "mode", split_axis=3, concat_axis=2, tiled=True)
    merged = moved.reshape(field.shape)
    merged = complex_product(merged, chosen[2], "sce,cd->sde")
    return complex_product(merged, chosen[3], "sce,ed->scd")[:, :, None]


def on_device(n, stem_tensor, branch_tensors, branch_order):
    _, stems, held, bw, _ = stem_tensor.shape
    rows = bw // n
    fits = stems == held == 1 and rows % 8 == 0 and 3 * rows <= LANES and n & (n - 1) == 0 and n * rows == bw
    if fits and bw % (4 * LANES) == 0:
        return fused(n, stem_tensor, branch_tensors, branch_order)
    return plain(stem_tensor, branch_tensors, branch_order)


def solution(mesh):
    return jax.shard_map(
        functools.partial(on_device, mesh.shape["mode"]),
        mesh=mesh,
        in_specs=(P(None, "cuts", "mode", None, None), P(), P()),
        out_specs=P(None, "cuts", "mode", None, None),
        check_vma=False,
    )
```

profile of v0, /device:TPU:8, one launch (start us, length us, event | category | flops | bytes accessed | tf_op | source)
XLA Modules:
  0.0 54.2 jit_solution(16361204420117940919)
XLA Ops:
  0.0 52.8 %shard_map.37 = f32[2,512,512]{2,1,0:T(8,128)S(1)} custom-call(s32[4]{0:T(128)} %order_ref.1, f32[2,512,512]{2,1,0:T(8,128)} %bitcast.5, f32[4,2,512,512]{3,2,1,0:T(8,128)} %branch_ref.1), custom_call_target="tpu_custom_call" | custom-call | tf_op jit(solution)/shard_map/pallas_call | solution.py:211
  52.8 1.3 %copy.6 = f32[2,1,1,512,512]{4,3,2,1,0:T(8,128)} copy(f32[2,1,1,512,512]{4,3,2,1,0:T(8,128)S(1)} %bitcast.4) | data formatting | bytes 4194304
where the time goes:
time: 55.1 us; the launch traced here: 54.2 us
  Pallas kernels  52.8 us (96%)
  local copies, waits for them, and re-layouts  1.32 us (2%)
    pallas_call x1, Pallas kernels, fused(): pl.pallas_call(functools.partial(kernel, n), out_shape=jax.ShapeDtypeStru...  52.8 us
    unnamed x1, local copies, waits for them, and re-layouts  1.32 us

commit v1 on v0

--- a/solution.py
+++ b/solution.py
@@ -43,7 +43,7 @@
 
 
 def kernel(n, order_ref, stem_ref, branch_ref, out_ref, stem, xh, xl, bh, bl, dh, dl, wh, wl,
-           lch, lcl, lct, sent, got, acc, load_sem, branch_sem, out_sem, send_sem, recv_sem, *branch):
+           lch, lcl, lct, sent, got, order, order_sem, stem_sem, left_sem, branch_sem, send_sem, recv_sem, left_0, left_1, *branch):
     bw = stem.shape[1]
     rows = bw // n
     per = LANES // rows
@@ -56,19 +56,26 @@
     def column(s):
         return pl.ds(pl.multiple_of(flip(z, s, groups) * LANES, LANES), LANES)
 
-    stem_copies = [pltpu.make_async_copy(stem_ref.at[part], stem.at[part], load_sem.at[part]) for part in range(2)]
-    branch_copies = {}
-    for s in sequence:
-        branch_copies[s] = pltpu.make_async_copy(branch_ref.at[:, :, :, column(s)], branch[s], branch_sem.at[s])
-        if s == sequence[0]:
-            branch_copies[s].start()
-    for copy in stem_copies:
-        copy.start()
-
     barrier = pltpu.get_barrier_semaphore()
-    for k in range(1, n):
+    for k in range(n - 1, 0, -1):
         pl.semaphore_signal(barrier, inc=1, device_id={"mode": flip(me, k, n)}, device_id_type=MESH)
-    o0, o1, o2, o3 = (order_ref[k] for k in range(4))
+
+    order_copy = pltpu.make_async_copy(order_ref, order, order_sem)
+    order_copy.start()
+    halves = [pl.ds(h * (bw // 2), bw // 2) for h in range(2)]
+    lead = sequence[0]
+    left, left_copies, stem_copies = (left_0, left_1), [], []
+    for h, half in enumerate(halves):
+        left_copies.append(pltpu.make_async_copy(
+            branch_ref.at[:, :, half, column(lead)], left[h], left_sem.at[h]))
+        stem_copies.append([
+            pltpu.make_async_copy(stem_ref.at[part, half], stem.at[part, half], stem_sem.at[part, h]) for part in range(2)])
+        for copy in [left_copies[h]] + stem_copies[h]:
+            copy.start()
+    branch_copies = {
+        s: pltpu.make_async_copy(branch_ref.at[:, :, :, column(s)], branch[s], branch_sem.at[s]) for s in sequence}
+    order_copy.wait()
+    o0, o1, o2, o3 = (order[k] for k in range(4))
 
     def left_rows(s):
         return jnp.concatenate([branch[s][o0, part].T for part in range(2)], axis=0)
@@ -92,23 +99,25 @@
         for k in range(per):
             own(s).start() if s == 0 and k == 0 else hop(s, k).start()
 
-    branch_copies[sequence[0]].wait()
-    high, low = split(left_rows(sequence[0]))
-    by = []
-    for part in range(2):
-        stem_copies[part].wait()
-        if part == 1:
-            for s in sequence[1:]:
-                branch_copies[s].start()
-        xh[part], xl[part] = split(stem[part])
-        by.append(dot3(high, low, xh[part], xl[part]))
+    by = [None, None]
+    for h, half in enumerate(halves):
+        left_copies[h].wait()
+        high, low = split(jnp.concatenate([left[h][o0, part].T for part in range(2)], axis=0))
+        for part in range(2):
+            stem_copies[h][part].wait()
+            if h == part == 1:
+                for s in sequence[1:] + [lead]:
+                    branch_copies[s].start()
+            xh[part, half], xl[part, half] = split(stem[part, half])
+            add = dot3(high, low, xh[part, half], xl[part, half])
+            by[part] = add if h == 0 else by[part] + add
     real, imag = by[0][:LANES] - by[1][LANES:], by[1][:LANES] + by[0][LANES:]
     pl.semaphore_wait(barrier, n - 1)
-    send(sequence[0], real, imag)
+    send(lead, real, imag)
     for s in early[1:]:
         branch_copies[s].wait()
         send(s, *first_rows(s))
-    for s in sequence[len(early):]:
+    for s in sequence[len(early):] + [lead]:
         branch_copies[s].wait()
 
     for s in range(groups):
@@ -168,6 +177,10 @@
     def arrive(s, j):
         pltpu.make_async_copy(got.at[s, j], got.at[s, j], recv_sem.at[s, j]).wait()
 
+    def result(i):
+        part, row = divmod(i * tile, bw)
+        return part, slice(row, row + tile)
+
     for index, s in enumerate(arrivals):
         places = [flip(q, k, per) if s == last else k for k in range(per)]
         if s == last:
@@ -182,18 +195,13 @@
         for i in range(2 * bw // tile):
             at = slice(i * tile, (i + 1) * tile)
             add = dot3(lch[s, at], lcl[s, at], right_high, right_low)
-            acc[at] = add if index == 0 else acc[at] + add
+            out_ref[result(i)] = add if index == 0 else out_ref[result(i)] + add
     arrive(last, final)
     high, low = split(jnp.concatenate([got[last, final, 0], got[last, final, 1]], axis=0))
     right = jnp.concatenate([high, low, high], axis=0)
     for i in range(2 * bw // tile):
         at = slice(i * tile, (i + 1) * tile)
-        acc[at] = acc[at] + dot(lct[at, : 6 * rows], right)
-        part, row = divmod(i * tile, bw)
-        pltpu.make_async_copy(acc.at[at], out_ref.at[part, pl.ds(row, tile)], out_sem.at[i]).start()
-    for i in range(2 * bw // tile):
-        part, row = divmod(i * tile, bw)
-        pltpu.make_async_copy(acc.at[pl.ds(i * tile, tile)], out_ref.at[part, pl.ds(row, tile)], out_sem.at[i]).wait()
+        out_ref[result(i)] = out_ref[result(i)] + dot(lct[at, : 6 * rows], right)
     for s in range(groups):
         for k in range(per):
             if s or k:
@@ -211,8 +219,8 @@
     return pl.pallas_call(
         functools.partial(kernel, n),
         out_shape=jax.ShapeDtypeStruct((2, bw, bw), F32),
-        in_specs=[pl.BlockSpec(memory_space=pltpu.SMEM)] + [pl.BlockSpec(memory_space=pl.ANY)] * 2,
-        out_specs=pl.BlockSpec(memory_space=pl.ANY),
+        in_specs=[pl.BlockSpec(memory_space=pl.ANY)] * 3,
+        out_specs=pl.BlockSpec(memory_space=pltpu.VMEM),
         scratch_shapes=[
             pltpu.VMEM((2, bw, bw), F32),
             *[square] * 8,
@@ -221,15 +229,17 @@
             pltpu.VMEM((2 * bw, 2 * LANES), BF16),
             pltpu.VMEM((groups, per, 2, rows, bw), F32),
             pltpu.VMEM((groups, per, 2, rows, bw), F32),
-            pltpu.VMEM((2 * bw, bw), F32),
+            pltpu.SMEM(branch_order.shape, jnp.int32),
+            pltpu.SemaphoreType.DMA,
+            pltpu.SemaphoreType.DMA((2, 2)),
             pltpu.SemaphoreType.DMA((2,)),
             pltpu.SemaphoreType.DMA((groups,)),
-            pltpu.SemaphoreType.DMA((bw // LANES,)),
             pltpu.SemaphoreType.DMA((groups, per)),
             pltpu.SemaphoreType.DMA((groups, per)),
+            *[pltpu.VMEM((4, 2, bw // 2, LANES), F32)] * 2,
             *[pltpu.VMEM((4, 2, bw, LANES), F32)] * groups,
         ],
-        compiler_params=pltpu.CompilerParams(collective_id=0, has_side_effects=True, vmem_limit_bytes=32 << 20),
+        compiler_params=pltpu.CompilerParams(collective_id=0, has_side_effects=True, vmem_limit_bytes=40 << 20),
     )(hbm(branch_order), hbm(stem_tensor.reshape(2, bw, bw)), hbm(branch_tensors)).reshape(stem_tensor.shape)
 
 

time: 55.1 us -> 53.4 us (0.969)
  Pallas kernels: 52.8 us -> 51.1 us
    pallas_call x1, Pallas kernels: 52.8 us -> 51.1 us  [fused(): pl.pallas_call(functools.partial(kernel, n), out_shape=jax.ShapeDtypeStru...]
where the time goes in v1:
time: 53.4 us; the launch traced here: 52.4 us
  Pallas kernels  51.1 us (96%)
  local copies, waits for them, and re-layouts  1.32 us (2%)
    pallas_call x1, Pallas kernels, fused(): pl.pallas_call(functools.partial(kernel, n), out_shape=jax.ShapeDtypeStru...  51.1 us
    unnamed x1, local copies, waits for them, and re-layouts  1.32 us

profile of v1, /device:TPU:8, one launch (start us, length us, event | category | flops | bytes accessed | tf_op | source)
XLA Modules:
  0.0 52.4 jit_solution(6135734549302356126)
XLA Ops:
  0.0 51.1 %shard_map.37 = f32[2,512,512]{2,1,0:T(8,128)S(1)} custom-call(s32[4]{0:T(128)} %order_ref.1, f32[2,512,512]{2,1,0:T(8,128)} %bitcast.5, f32[4,2,512,512]{3,2,1,0:T(8,128)} %branch_ref.1), custom_call_target="tpu_custom_call" | custom-call | tf_op jit(solution)/shard_map/pallas_call | solution.py:219
  51.1 1.3 %copy.6 = f32[2,1,1,512,512]{4,3,2,1,0:T(8,128)} copy(f32[2,1,1,512,512]{4,3,2,1,0:T(8,128)S(1)} %bitcast.4) | data formatting | bytes 4194304

commit v2 on v1

--- a/solution.py
+++ b/solution.py
@@ -21,6 +21,14 @@
     return result
 
 
+def xor(a, b, size):
+    result, bit = 0, 1
+    while bit < size:
+        result = result + lax.rem(lax.div(a, bit) + lax.div(b, bit), 2) * bit
+        bit *= 2
+    return result
+
+
 def split(value):
     high = value.astype(BF16)
     return high, (value - high.astype(F32)).astype(BF16)
@@ -42,16 +50,18 @@
     return by_real[:m] - by_imag[m:], by_imag[:m] + by_real[m:]
 
 
-def kernel(n, order_ref, stem_ref, branch_ref, out_ref, stem, xh, xl, bh, bl, dh, dl, wh, wl,
-           lch, lcl, lct, sent, got, order, order_sem, stem_sem, left_sem, branch_sem, send_sem, recv_sem, left_0, left_1, *branch):
+def kernel(n, order_ref, stem_ref, branch_ref, out_ref, lct, right_ref, stem, xh, xl, bh, bl, dh, dl, wh, wl,
+           lch, lcl, lce, sent, got, order, order_sem, stem_sem, left_sem, branch_sem, send_sem, recv_sem, left_0, left_1, *branch):
     bw = stem.shape[1]
     rows = bw // n
     per = LANES // rows
     groups = n // per
     me = lax.axis_index("mode")
     z, q = lax.div(me, per), lax.rem(me, per)
+    upper = lax.div(q, per // 2)
     sequence = [groups // 2] + [s for s in range(1, groups) if s != groups // 2] + [0]
     early = sequence[: groups // 2]
+    lead, last = sequence[0], sequence[-2]
 
     def column(s):
         return pl.ds(pl.multiple_of(flip(z, s, groups) * LANES, LANES), LANES)
@@ -63,7 +73,6 @@
     order_copy = pltpu.make_async_copy(order_ref, order, order_sem)
     order_copy.start()
     halves = [pl.ds(h * (bw // 2), bw // 2) for h in range(2)]
-    lead = sequence[0]
     left, left_copies, stem_copies = (left_0, left_1), [], []
     for h, half in enumerate(halves):
         left_copies.append(pltpu.make_async_copy(
@@ -83,37 +92,49 @@
     def first_rows(s):
         return complex_rows(left_rows(s), xh, xl)
 
-    def hop(s, k):
-        j = flip(q, k, per)
+    def partner(s, i):
+        if s == lead:
+            return i
+        return xor(q, lax.rem(i + upper, per), per) if s == last else flip(q, i, per)
+
+    def hop(s, i):
+        j = partner(s, i)
         return pltpu.make_async_remote_copy(
-            src_ref=sent.at[s, j], dst_ref=got.at[s, q], send_sem=send_sem.at[s, k], recv_sem=recv_sem.at[s, q],
+            src_ref=sent.at[s, j], dst_ref=got.at[s, q], send_sem=send_sem.at[s, i], recv_sem=recv_sem.at[s, q],
             device_id={"mode": flip(z, s, groups) * per + j}, device_id_type=MESH)
 
     def own(s):
         return pltpu.make_async_copy(sent.at[s, q], got.at[s, q], recv_sem.at[s, q])
 
-    def send(s, real, imag):
-        for j in range(per):
-            sent[s, j, 0] = real[j * rows:(j + 1) * rows]
-            sent[s, j, 1] = imag[j * rows:(j + 1) * rows]
-        for k in range(per):
-            own(s).start() if s == 0 and k == 0 else hop(s, k).start()
-
+    def send(s, real, imag, which=range(per)):
+        for place, j in enumerate(which):
+            sent[s, j, 0] = real[place * rows:(place + 1) * rows]
+            sent[s, j, 1] = imag[place * rows:(place + 1) * rows]
+        for i in which:
+            own(s).start() if s == 0 and i == 0 else hop(s, i).start()
+
+    highs, lows = [], []
+    part_rows = LANES // 2
     by = [None, None]
     for h, half in enumerate(halves):
         left_copies[h].wait()
-        high, low = split(jnp.concatenate([left[h][o0, part].T for part in range(2)], axis=0))
+        high, low = split(jnp.concatenate(
+            [left[h][o0, part].T[m * part_rows:(m + 1) * part_rows] for m in range(2) for part in range(2)], axis=0))
+        highs.append(high)
+        lows.append(low)
         for part in range(2):
             stem_copies[h][part].wait()
             if h == part == 1:
                 for s in sequence[1:] + [lead]:
                     branch_copies[s].start()
             xh[part, half], xl[part, half] = split(stem[part, half])
-            add = dot3(high, low, xh[part, half], xl[part, half])
+            add = dot3(high[:LANES], low[:LANES], xh[part, half], xl[part, half])
             by[part] = add if h == 0 else by[part] + add
-    real, imag = by[0][:LANES] - by[1][LANES:], by[1][:LANES] + by[0][LANES:]
     pl.semaphore_wait(barrier, n - 1)
-    send(lead, real, imag)
+    send(lead, by[0][:part_rows] - by[1][part_rows:], by[1][:part_rows] + by[0][part_rows:], range(per // 2))
+    high, low = (jnp.concatenate([piece[LANES:] for piece in pieces], axis=1) for pieces in (highs, lows))
+    by = [dot3(high, low, xh[part], xl[part]) for part in range(2)]
+    send(lead, by[0][:part_rows] - by[1][part_rows:], by[1][:part_rows] + by[0][part_rows:], range(per // 2, per))
     for s in early[1:]:
         branch_copies[s].wait()
         send(s, *first_rows(s))
@@ -141,35 +162,35 @@
         real, imag = first_rows(s)
         send(s, *complex_rows(jnp.concatenate([real, imag], axis=0), wh, wl))
 
-    last = sequence[-2]
-
     def third_rows(t, part, s):
         if s != last:
             return branch[t][o2, part, column(s), :]
         base = flip(z, s, groups) * LANES
         return jnp.concatenate([
-            branch[t][o2, part, pl.ds(pl.multiple_of(base + flip(q, k, per) * rows, rows), rows), :]
-            for k in range(per)], axis=0)
-
+            branch[t][o2, part, pl.ds(pl.multiple_of(base + partner(s, i) * rows, rows), rows), :]
+            for i in range(per)], axis=0)
+
+    pairs = ((lce, 0, LANES - 2 * rows), (lct, LANES - 2 * rows, LANES))
     for s in range(groups):
         for t in range(groups):
             real, imag = (split(third_rows(t, part, s).T) for part in range(2))
             top = column(t)
             low_half = pl.ds(pl.multiple_of(bw + flip(z, t, groups) * LANES, LANES), LANES)
-            for ref, r, i in ((lch, real[0], imag[0]), (lcl, real[1], imag[1])):
-                ref[s, top, :LANES] = r
-                ref[s, top, LANES:] = -i
-                ref[s, low_half, :LANES] = i
-                ref[s, low_half, LANES:] = r
-            if s == last:
-                tail = slice(LANES - rows, LANES)
+            if s != last:
+                for ref, r, i in ((lch, real[0], imag[0]), (lcl, real[1], imag[1])):
+                    ref[s, top, :LANES] = r
+                    ref[s, top, LANES:] = -i
+                    ref[s, low_half, :LANES] = i
+                    ref[s, low_half, LANES:] = r
+                continue
+            for ref, begin, end in pairs:
                 for place, (r, i) in enumerate(((real[0], imag[0]), (real[0], imag[0]), (real[1], imag[1]))):
-                    at = slice(2 * place * rows, (2 * place + 1) * rows)
-                    after = slice((2 * place + 1) * rows, (2 * place + 2) * rows)
-                    lct[top, at] = r[:, tail]
-                    lct[top, after] = -i[:, tail]
-                    lct[low_half, at] = i[:, tail]
-                    lct[low_half, after] = r[:, tail]
+                    at = slice(2 * place * (end - begin), (2 * place + 1) * (end - begin))
+                    after = slice((2 * place + 1) * (end - begin), (2 * place + 2) * (end - begin))
+                    ref[top, at] = r[:, begin:end]
+                    ref[top, after] = -i[:, begin:end]
+                    ref[low_half, at] = i[:, begin:end]
+                    ref[low_half, after] = r[:, begin:end]
 
     arrivals = [0] + [s for s in early if s != groups // 2] + [groups // 2] + [s for s in sequence[len(early):] if s]
     tile = 2 * LANES
@@ -181,31 +202,45 @@
         part, row = divmod(i * tile, bw)
         return part, slice(row, row + tile)
 
+    def stacked(places):
+        for i in places:
+            arrive(last, partner(last, i))
+        high, low = split(jnp.concatenate([got[last, partner(last, i), part] for part in range(2) for i in places], axis=0))
+        return jnp.concatenate([high, low, high], axis=0)
+
     for index, s in enumerate(arrivals):
-        places = [flip(q, k, per) if s == last else k for k in range(per)]
         if s == last:
-            final = places.pop()
-        for j in places:
-            arrive(s, j)
-        blank = [jnp.zeros((rows, bw), F32)] * (per - len(places))
-        arrived = jnp.concatenate([piece for part in range(2) for piece in [got[s, j, part] for j in places] + blank], axis=0)
-        if s in early:
-            arrived = jnp.concatenate(complex_rows(arrived, wh, wl), axis=0)
-        right_high, right_low = split(arrived)
+            right = stacked(range(per - 2))
+        else:
+            for j in range(per):
+                arrive(s, j)
+            arrived = jnp.concatenate([got[s, j, part] for part in range(2) for j in range(per)], axis=0)
+            if s in early:
+                arrived = jnp.concatenate(complex_rows(arrived, wh, wl), axis=0)
+            right_high, right_low = split(arrived)
         for i in range(2 * bw // tile):
             at = slice(i * tile, (i + 1) * tile)
-            add = dot3(lch[s, at], lcl[s, at], right_high, right_low)
+            add = dot(lce[at], right) if s == last else dot3(lch[s, at], lcl[s, at], right_high, right_low)
             out_ref[result(i)] = add if index == 0 else out_ref[result(i)] + add
-    arrive(last, final)
-    high, low = split(jnp.concatenate([got[last, final, 0], got[last, final, 1]], axis=0))
-    right = jnp.concatenate([high, low, high], axis=0)
-    for i in range(2 * bw // tile):
+    for s in range(groups):
+        for i in range(per):
+            if s or i:
+                hop(s, i).wait_send()
+    right_ref[...] = stacked(range(per - 2, per))
+
+
+def finish(acc_ref, left_ref, right_ref, out_ref, tiles, sem):
+    count, tile, bw = tiles.shape
+    right = right_ref[...]
+    copies = []
+    for i in range(count):
+        part, row = divmod(i * tile, bw)
         at = slice(i * tile, (i + 1) * tile)
-        out_ref[result(i)] = out_ref[result(i)] + dot(lct[at, : 6 * rows], right)
-    for s in range(groups):
-        for k in range(per):
-            if s or k:
-                hop(s, k).wait_send()
+        tiles[i] = acc_ref[part, row:row + tile] + dot(left_ref[at], right)
+        copies.append(pltpu.make_async_copy(tiles.at[i], out_ref.at[part, pl.ds(row, tile)], sem.at[i]))
+        copies[i].start()
+    for copy in copies:
+        copy.wait()
 
 
 def fused(n, stem_tensor, branch_tensors, branch_order):
@@ -216,17 +251,23 @@
     square = pltpu.VMEM((2, bw, bw), BF16)
     hbm = functools.partial(pltpu.with_memory_space_constraint, memory_space=pltpu.HBM)
     window = pltpu.VMEM((groups, 2 * bw, 2 * LANES), BF16)
-    return pl.pallas_call(
+    vmem = pl.BlockSpec(memory_space=pltpu.VMEM)
+    tiles = 2 * bw // LANES
+    partial = pl.pallas_call(
         functools.partial(kernel, n),
-        out_shape=jax.ShapeDtypeStruct((2, bw, bw), F32),
+        out_shape=[
+            jax.ShapeDtypeStruct((2, bw, bw), F32),
+            jax.ShapeDtypeStruct((2 * bw, 12 * rows), BF16),
+            jax.ShapeDtypeStruct((12 * rows, bw), BF16),
+        ],
         in_specs=[pl.BlockSpec(memory_space=pl.ANY)] * 3,
-        out_specs=pl.BlockSpec(memory_space=pltpu.VMEM),
+        out_specs=[vmem] * 3,
         scratch_shapes=[
             pltpu.VMEM((2, bw, bw), F32),
             *[square] * 8,
             window,
             window,
-            pltpu.VMEM((2 * bw, 2 * LANES), BF16),
+            pltpu.VMEM((2 * bw, 6 * (LANES - 2 * rows)), BF16),
             pltpu.VMEM((groups, per, 2, rows, bw), F32),
             pltpu.VMEM((groups, per, 2, rows, bw), F32),
             pltpu.SMEM(branch_order.shape, jnp.int32),
@@ -240,7 +281,15 @@
             *[pltpu.VMEM((4, 2, bw, LANES), F32)] * groups,
         ],
         compiler_params=pltpu.CompilerParams(collective_id=0, has_side_effects=True, vmem_limit_bytes=40 << 20),
-    )(hbm(branch_order), hbm(stem_tensor.reshape(2, bw, bw)), hbm(branch_tensors)).reshape(stem_tensor.shape)
+    )(hbm(branch_order), hbm(stem_tensor.reshape(2, bw, bw)), hbm(branch_tensors))
+    return pl.pallas_call(
+        finish,
+        out_shape=jax.ShapeDtypeStruct((2, bw, bw), F32),
+        in_specs=[vmem] * 3,
+        out_specs=pl.BlockSpec(memory_space=pl.ANY),
+        scratch_shapes=[pltpu.VMEM((tiles, LANES, bw), F32), pltpu.SemaphoreType.DMA((tiles,))],
+        compiler_params=pltpu.CompilerParams(vmem_limit_bytes=8 << 20),
+    )(*partial).reshape(stem_tensor.shape)
 
 
 def complex_product(first, second, form):

time: 53.4 us -> 52.3 us (0.979)
  the two profiles are of different devices: /device:TPU:8 before, /device:TPU:13 now
where the time goes in v2:
time: 52.3 us; the launch traced here: 52.1 us
  Pallas kernels  52.1 us (100%)
    pallas_call x1, Pallas kernels, fused(): pl.pallas_call(functools.partial(kernel, n), out_shape=[jax.ShapeDtypeStr...  50.5 us
    pallas_call x1, Pallas kernels, fused(): pl.pallas_call(finish, out_shape=jax.ShapeDtypeStruct((2, bw, bw), F32),...  1.61 us

profile of v2, /device:TPU:13, one launch (start us, length us, event | category | flops | bytes accessed | tf_op | source)
XLA Modules:
  0.0 52.1 jit_solution(15108462450932191525)
XLA Ops:
  0.0 50.5 %shard_map.37 = (f32[2,512,512]{2,1,0:T(8,128)S(1)}, bf16[1024,384]{1,0:T(8,128)(2,1)S(1)}, bf16[384,512]{1,0:T(8,128)(2,1)S(1)}) custom-call(s32[4]{0:T(128)} %order_ref.1, f32[2,512,512]{2,1,0:T(8,128)} %bitcast.4, f32[4,2,512,512]{3,2,1,0:T(8,128)} %branch_ref.1), custom_call_target="tpu_custom_call" | custom-call | tf_op jit(solution)/shard_map/pallas_call | solution.py:256
  50.5 1.6 %shard_map.38 = f32[2,512,512]{2,1,0:T(8,128)} custom-call(f32[2,512,512]{2,1,0:T(8,128)S(1)} %get-tuple-element.8.acc_ref, bf16[1024,384]{1,0:T(8,128)(2,1)S(1)} %get-tuple-element.9.left_ref, bf16[384,512]{1,0:T(8,128)(2,1)S(1)} %get-tuple-element.10.right_ref), custom_call_target="tpu_custom_call" | custom-call | tf_op jit(solution)/shard_map/pallas_call | solution.py:285

commit v3 on v2

v3 whole, which is shorter than its diff:
```python
import functools

import jax
import jax.numpy as jnp
from jax import lax
from jax.experimental import pallas as pl
from jax.experimental.pallas import tpu as pltpu
from jax.sharding import PartitionSpec as P

MESH = pl.DeviceIdType.MESH
LANES = 128
HEAD = 1
F32, BF16 = jnp.float32, jnp.bfloat16


def flip(value, mask, size):
    result, bit = 0, 1
    while bit < size:
        digit = lax.rem(lax.div(value, bit), 2)
        result = result + (1 - digit if (mask // bit) % 2 else digit) * bit
        bit *= 2
    return result


def split(value):
    high = value.astype(BF16)
    return high, (value - high.astype(F32)).astype(BF16)


def dot(a, b):
    return jnp.dot(a, b, preferred_element_type=F32)


def dot3(high, low, right_high, right_low):
    return dot(high, right_high) + (dot(high, right_low) + dot(low, right_high))


def complex_rows(rows, right_high, right_low):
    m = rows.shape[0] // 2
    high, low = split(rows)
    by_real = dot3(high, low, right_high[0], right_low[0])
    by_imag = dot3(high, low, right_high[1], right_low[1])
    return by_real[:m] - by_imag[m:], by_imag[:m] + by_real[m:]


def kernel(n, order_ref, stem_ref, branch_ref, out_ref, last_high, last_low, tail_high, tail_low, stem, xh, xl, bh, bl, dh, dl, wh, wl,
           lch, lcl, sent, got, order, order_sem, stem_sem, left_sem, branch_sem, send_sem, recv_sem, last_sem, left_0, left_1, *branch):
    bw = stem.shape[1]
    rows = bw // n
    per = LANES // rows
    groups = n // per
    me = lax.axis_index("mode")
    z, q = lax.div(me, per), lax.rem(me, per)
    upper = lax.div(q, per // 2)
    sequence = [groups // 2] + [s for s in range(1, groups) if s != groups // 2] + [0]
    early = sequence[: groups // 2]
    lead, last = sequence[0], sequence[-2]

    def column(s):
        return pl.ds(pl.multiple_of(flip(z, s, groups) * LANES, LANES), LANES)

    barrier = pltpu.get_barrier_semaphore()
    for k in range(n - 1, 0, -1):
        pl.semaphore_signal(barrier, inc=1, device_id={"mode": flip(me, k, n)}, device_id_type=MESH)

    order_copy = pltpu.make_async_copy(order_ref, order, order_sem)
    order_copy.start()
    halves = [pl.ds(h * (bw // 2), bw // 2) for h in range(2)]
    left = (left_0, left_1)
    left_copies = [pltpu.make_async_copy(
        branch_ref.at[:, :, half, column(lead)], left[h], left_sem.at[h]) for h, half in enumerate(halves)]
    stem_copies = [[pltpu.make_async_copy(
        stem_ref.at[part, half], stem.at[part, half], stem_sem.at[part, h]) for part in range(2)] for h, half in enumerate(halves)]
    for copy in (left_copies[0], *stem_copies[0], left_copies[1], *stem_copies[1]):
        copy.start()
    branch_copies = {
        s: pltpu.make_async_copy(branch_ref.at[:, :, :, column(s)], branch[s], branch_sem.at[s]) for s in sequence}
    order_copy.wait()
    o0, o1, o2, o3 = (order[k] for k in range(4))

    def left_rows(s):
        return jnp.concatenate([branch[s][o0, part].T for part in range(2)], axis=0)

    def first_rows(s):
        return complex_rows(left_rows(s), xh, xl)

    def partner(s, i):
        if s == lead:
            return i
        if s != last:
            return flip(q, i, per)
        column = upper if i >= per // 2 else 1 - upper
        return column * (per // 2) + (per - 1 - i) % (per // 2)

    def hop(s, i, h=None):
        j = partner(s, i)
        where = () if h is None else (slice(None), slice(None), halves[h])
        return pltpu.make_async_remote_copy(
            src_ref=sent.at[(s, j, *where)], dst_ref=got.at[(s, q, *where)], send_sem=send_sem.at[s],
            recv_sem=recv_sem.at[s] if h is None else last_sem.at[h],
            device_id={"mode": flip(z, s, groups) * per + j}, device_id_type=MESH)

    def own(s):
        return pltpu.make_async_copy(sent.at[s, q], got.at[s, q], recv_sem.at[s])

    def send(s, real, imag, which=range(per)):
        for place, j in enumerate(which):
            sent[s, j, 0] = real[place * rows:(place + 1) * rows]
            sent[s, j, 1] = imag[place * rows:(place + 1) * rows]
        for h in range(2) if s == last else [None]:
            for i in which:
                own(s).start() if s == 0 and i == 0 else hop(s, i, h).start()

    highs, lows = [], []
    parcels = [range(HEAD), range(HEAD, per)]
    cut = 2 * HEAD * rows
    by = [None, None]

    def send_lead(by, which):
        m = by[0].shape[0] // 2
        send(lead, by[0][:m] - by[1][m:], by[1][:m] + by[0][m:], which)

    for h, half in enumerate(halves):
        left_copies[h].wait()
        high, low = split(jnp.concatenate([
            left[h][o0, part].T[which[0] * rows:(which[-1] + 1) * rows] for which in parcels for part in range(2)], axis=0))
        highs.append(high)
        lows.append(low)
        for part in range(2):
            stem_copies[h][part].wait()
            if h == part == 1:
                for s in sequence[1:] + [lead]:
                    branch_copies[s].start()
            xh[part, half], xl[part, half] = split(stem[part, half])
            both_parts = dot(jnp.concatenate([high[:cut], low[:cut]], axis=0), xh[part, half])
            add = both_parts[:cut] + (both_parts[cut:] + dot(high[:cut], xl[part, half]))
            by[part] = add if h == 0 else by[part] + add
    pl.semaphore_wait(barrier, n - 1)
    send_lead(by, parcels[0])
    high, low = (jnp.concatenate([piece[cut:] for piece in pieces], axis=1) for pieces in (highs, lows))
    send_lead([dot3(high, low, xh[part], xl[part]) for part in range(2)], parcels[1])
    for s in early[1:]:
        branch_copies[s].wait()
        send(s, *first_rows(s))
    for s in sequence[len(early):] + [lead]:
        branch_copies[s].wait()

    for s in range(groups):
        for part in range(2):
            bh[part, :, column(s)], bl[part, :, column(s)] = split(branch[s][o1, part])
            dh[part, :, column(s)], dl[part, :, column(s)] = split(branch[s][o3, part])

    def both(i, carry):
        at = pl.ds(pl.multiple_of(i * LANES, LANES), LANES)
        high = jnp.concatenate([bh[0, at], bh[1, at]], axis=0)
        low = jnp.concatenate([bl[0, at], bl[1, at]], axis=0)
        by_real = dot3(high, low, dh[0], dl[0])
        by_imag = dot3(high, low, dh[1], dl[1])
        wh[0, at], wl[0, at] = split(by_real[:LANES] - by_imag[LANES:])
        wh[1, at], wl[1, at] = split(by_imag[:LANES] + by_real[LANES:])
        return carry

    lax.fori_loop(0, bw // LANES, both, 0)

    for s in sequence[len(early):]:
        real, imag = first_rows(s)
        send(s, *complex_rows(jnp.concatenate([real, imag], axis=0), wh, wl))

    for s in range(groups):
        high_ref, low_ref = (last_high, last_low) if s == last else (lch.at[s], lcl.at[s])
        for t in range(groups):
            real, imag = (split(branch[t][o2, part, column(s), :].T) for part in range(2))
            top = column(t)
            low_half = pl.ds(pl.multiple_of(bw + flip(z, t, groups) * LANES, LANES), LANES)
            for ref, r, i in ((high_ref, real[0], imag[0]), (low_ref, real[1], imag[1])):
                ref[top, :LANES] = r
                ref[top, LANES:] = -i
                ref[low_half, :LANES] = i
                ref[low_half, LANES:] = r

    arrivals = [0] + [s for s in early if s != groups // 2] + [groups // 2] + [s for s in sequence[len(early):] if s]
    tile = 2 * LANES

    def await_bytes(place, sem):
        pltpu.make_async_copy(place, place, sem).wait()

    def arrived(s, side):
        return jnp.concatenate([got[s, j, part, :, side] for part in range(2) for j in range(per)], axis=0)

    for index, s in enumerate(arrivals):
        if s == last:
            await_bytes(got.at[last, :, :, :, halves[0]], last_sem.at[0])
            side = slice(0, bw // 2)
        else:
            await_bytes(got.at[s], recv_sem.at[s])
            side = slice(0, bw)
        right = arrived(s, side)
        if s in early:
            right = jnp.concatenate(complex_rows(right, wh, wl), axis=0)
        right_high, right_low = split(right)
        high_ref, low_ref = (last_high, last_low) if s == last else (lch.at[s], lcl.at[s])
        for i in range(2 * bw // tile):
            at = slice(i * tile, (i + 1) * tile)
            part, row = divmod(i * tile, bw)
            place = (part, slice(row, row + tile), side)
            add = dot3(high_ref[at], low_ref[at], right_high, right_low)
            out_ref[place] = add if index == 0 else out_ref[place] + add
    for s in range(groups):
        await_bytes(sent.at[s, pl.ds(0, per if s else per - 1)], send_sem.at[s])
    await_bytes(got.at[last, :, :, :, halves[1]], last_sem.at[1])
    tail_high[...], tail_low[...] = split(arrived(last, slice(bw // 2, bw)))


def finish(acc_ref, high_ref, low_ref, right_high, right_low, out_ref, tiles, side_sem, sem):
    count, tile, half = tiles.shape
    copies = []
    for part in range(2):
        at = (part, slice(None), pl.ds(0, half))
        copies.append(pltpu.make_async_copy(acc_ref.at[at], out_ref.at[at], side_sem.at[part]))
        copies[part].start()
    right = right_high[...], right_low[...]
    for i in range(count):
        part, row = divmod(i * tile, 2 * half)
        at = slice(i * tile, (i + 1) * tile)
        tiles[i] = acc_ref[part, row:row + tile, half:] + dot3(high_ref[at], low_ref[at], *right)
        copies.append(pltpu.make_async_copy(tiles.at[i], out_ref.at[part, pl.ds(row, tile), pl.ds(half, half)], sem.at[i]))
        copies[-1].start()
    for copy in copies:
        copy.wait()


def fused(n, stem_tensor, branch_tensors, branch_order):
    bw = stem_tensor.shape[-1]
    rows = bw // n
    per = LANES // rows
    groups = n // per
    square = pltpu.VMEM((2, bw, bw), BF16)
    hbm = functools.partial(pltpu.with_memory_space_constraint, memory_space=pltpu.HBM)
    window = pltpu.VMEM((groups, 2 * bw, 2 * LANES), BF16)
    vmem = pl.BlockSpec(memory_space=pltpu.VMEM)
    tiles = 2 * bw // LANES
    partial = pl.pallas_call(
        functools.partial(kernel, n),
        out_shape=[
            jax.ShapeDtypeStruct((2, bw, bw), F32),
            *[jax.ShapeDtypeStruct((2 * bw, 2 * LANES), BF16)] * 2,
            *[jax.ShapeDtypeStruct((2 * LANES, bw // 2), BF16)] * 2,
        ],
        in_specs=[pl.BlockSpec(memory_space=pl.ANY)] * 3,
        out_specs=[vmem] * 5,
        scratch_shapes=[
            pltpu.VMEM((2, bw, bw), F32),
            *[square] * 8,
            window,
            window,
            pltpu.VMEM((groups, per, 2, rows, bw), F32),
            pltpu.VMEM((groups, per, 2, rows, bw), F32),
            pltpu.SMEM(branch_order.shape, jnp.int32),
            pltpu.SemaphoreType.DMA,
            pltpu.SemaphoreType.DMA((2, 2)),
            pltpu.SemaphoreType.DMA((2,)),
            pltpu.SemaphoreType.DMA((groups,)),
            pltpu.SemaphoreType.DMA((groups,)),
            pltpu.SemaphoreType.DMA((groups,)),
            pltpu.SemaphoreType.DMA((2,)),
            *[pltpu.VMEM((4, 2, bw // 2, LANES), F32)] * 2,
            *[pltpu.VMEM((4, 2, bw, LANES), F32)] * groups,
        ],
        compiler_params=pltpu.CompilerParams(collective_id=0, has_side_effects=True, vmem_limit_bytes=40 << 20),
    )(hbm(branch_order), hbm(stem_tensor.reshape(2, bw, bw)), hbm(branch_tensors))
    return pl.pallas_call(
        finish,
        out_shape=jax.ShapeDtypeStruct((2, bw, bw), F32),
        in_specs=[vmem] * 5,
        out_specs=pl.BlockSpec(memory_space=pl.ANY),
        scratch_shapes=[pltpu.VMEM((tiles, LANES, bw // 2), F32), pltpu.SemaphoreType.DMA((2,)), pltpu.SemaphoreType.DMA((tiles,))],
        compiler_params=pltpu.CompilerParams(vmem_limit_bytes=8 << 20),
    )(*partial).reshape(stem_tensor.shape)


def complex_product(first, second, form):
    high = lax.Precision.HIGHEST
    real = jnp.einsum(form, first[0], second[0], precision=high) - jnp.einsum(form, first[1], second[1], precision=high)
    imag = jnp.einsum(form, first[0], second[1], precision=high) + jnp.einsum(form, first[1], second[0], precision=high)
    return jnp.stack([real, imag])


def plain(stem_tensor, branch_tensors, branch_order):
    field = stem_tensor[:, :, 0]
    chosen = [branch_tensors[branch_order[index]] for index in range(4)]
    field = complex_product(field, chosen[0], "sce,cd->sde")
    field = complex_product(field, chosen[1], "sce,ed->scd")
    moved = lax.all_to_all(field[:, :, None], "mode", split_axis=3, concat_axis=2, tiled=True)
    merged = moved.reshape(field.shape)
    merged = complex_product(merged, chosen[2], "sce,cd->sde")
    return complex_product(merged, chosen[3], "sce,ed->scd")[:, :, None]


def on_device(n, stem_tensor, branch_tensors, branch_order):
    _, stems, held, bw, _ = stem_tensor.shape
    rows = bw // n
    fits = stems == held == 1 and rows % 8 == 0 and 3 * rows <= LANES and n & (n - 1) == 0 and n * rows == bw
    if fits and bw % (4 * LANES) == 0:
        return fused(n, stem_tensor, branch_tensors, branch_order)
    return plain(stem_tensor, branch_tensors, branch_order)


def solution(mesh):
    return jax.shard_map(
        functools.partial(on_device, mesh.shape["mode"]),
        mesh=mesh,
        in_specs=(P(None, "cuts", "mode", None, None), P(), P()),
        out_specs=P(None, "cuts", "mode", None, None),
        check_vma=False,
    )
```

time: 52.3 us -> 51.9 us (level)
  the two profiles are of different devices: /device:TPU:13 before, /device:TPU:8 now
where the time goes in v3:
time: 51.9 us; the launch traced here: 51.8 us
  Pallas kernels  51.7 us (100%)
    pallas_call x1, Pallas kernels, fused(): pl.pallas_call(functools.partial(kernel, n), out_shape=[jax.ShapeDtypeStr...  50.3 us
    pallas_call x1, Pallas kernels, fused(): pl.pallas_call(finish, out_shape=jax.ShapeDtypeStruct((2, bw, bw), F32),...  1.4 us

profile of v3, /device:TPU:8, one launch (start us, length us, event | category | flops | bytes accessed | tf_op | source)
XLA Modules:
  0.0 51.8 jit_solution(12827795103141003163)
XLA Ops:
  0.0 50.3 %shard_map.37 = (f32[2,512,512]{2,1,0:T(8,128)S(1)}, bf16[1024,256]{1,0:T(8,128)(2,1)S(1)}, bf16[1024,256]{1,0:T(8,128)(2,1)S(1)}, bf16[256,256]{1,0:T(8,128)(2,1)S(1)}, bf16[256,256]{1,0:T(8,128)(2,1)S(1)}) custom-call(s32[4]{0:T(128)} %order_ref.1, f32[2,512,512]{2,1,0:T(8,128)} %bitcast.4, f32[4,2,512,512]{3,2,1,0:T(8,128)} %branch_ref.1), custom_call_target="tpu_custom_call" | custom-call | tf_op jit(solution)/shard_map/pallas_call | solution.py:242
  50.4 1.4 %shard_map.38 = f32[2,512,512]{2,1,0:T(8,128)} custom-call(f32[2,512,512]{2,1,0:T(8,128)S(1)} %get-tuple-element.10.acc_ref, bf16[1024,256]{1,0:T(8,128)(2,1)S(1)} %get-tuple-element.11.high_ref, bf16[1024,256]{1,0:T(8,128)(2,1)S(1)} %get-tuple-element.12.low_ref, bf16[256,256]{1,0:T(8,128)(2,1)S(1)} %get-tuple-element.13.right_high, ...), custom_call_target="tpu_custom_call" | custom-call | tf_op jit(solution)/shard_map/pallas_call | solution.py:271

commit v4 on v3

--- a/solution.py
+++ b/solution.py
@@ -9,7 +9,6 @@
 
 MESH = pl.DeviceIdType.MESH
 LANES = 128
-HEAD = 1
 F32, BF16 = jnp.float32, jnp.bfloat16
 
 
@@ -44,7 +43,7 @@
 
 
 def kernel(n, order_ref, stem_ref, branch_ref, out_ref, last_high, last_low, tail_high, tail_low, stem, xh, xl, bh, bl, dh, dl, wh, wl,
-           lch, lcl, sent, got, order, order_sem, stem_sem, left_sem, branch_sem, send_sem, recv_sem, last_sem, left_0, left_1, *branch):
+           lch, lcl, sent, got, order, order_sem, stem_sem, left_sem, branch_sem, send_sem, recv_sem, last_sem, side_sem, notice_low, notice_top, left_0, left_1, *branch):
     bw = stem.shape[1]
     rows = bw // n
     per = LANES // rows
@@ -60,8 +59,30 @@
         return pl.ds(pl.multiple_of(flip(z, s, groups) * LANES, LANES), LANES)
 
     barrier = pltpu.get_barrier_semaphore()
-    for k in range(n - 1, 0, -1):
-        pl.semaphore_signal(barrier, inc=1, device_id={"mode": flip(me, k, n)}, device_id_type=MESH)
+    top, middle = groups - 1, groups // 2
+    near = middle ^ top
+
+    def greet(sem, s, k):
+        pl.semaphore_signal(
+            sem, inc=1, device_id={"mode": flip(z, s, groups) * per + flip(q, k, per)}, device_id_type=MESH)
+
+    for s in range(groups - 1, -1, -1):
+        for k in range(per):
+            if s == near:
+                pl.when(z != top)(functools.partial(greet, barrier, s, k))
+            elif s == lead:
+                pl.when(z + upper != top + 1)(functools.partial(greet, barrier, s, k))
+            elif s or k:
+                greet(barrier, s, k)
+
+    def equal(a, b):
+        return (a == b).astype(jnp.int32)
+
+    def enter():
+        pl.semaphore_wait(barrier, n - 1 - per * equal(z, middle) - per // 2 * equal(z, middle - 1))
+        for k in range(per):
+            pl.when(z == top)(functools.partial(greet, notice_low, near, k))
+            pl.when(z + upper == top + 1)(functools.partial(greet, notice_top, lead, k))
 
     order_copy = pltpu.make_async_copy(order_ref, order, order_sem)
     order_copy.start()
@@ -69,9 +90,10 @@
     left = (left_0, left_1)
     left_copies = [pltpu.make_async_copy(
         branch_ref.at[:, :, half, column(lead)], left[h], left_sem.at[h]) for h, half in enumerate(halves)]
-    stem_copies = [[pltpu.make_async_copy(
-        stem_ref.at[part, half], stem.at[part, half], stem_sem.at[part, h]) for part in range(2)] for h, half in enumerate(halves)]
-    for copy in (left_copies[0], *stem_copies[0], left_copies[1], *stem_copies[1]):
+    stem_copies = [pltpu.make_async_copy(
+        stem_ref.at[:, half, halves[0]], stem.at[:, half, halves[0]], stem_sem.at[k]) for k, half in enumerate(halves)]
+    side_copy = pltpu.make_async_copy(stem_ref.at[:, :, halves[1]], stem.at[:, :, halves[1]], side_sem)
+    for copy in (left_copies[0], stem_copies[0], left_copies[1], stem_copies[1], side_copy):
         copy.start()
     branch_copies = {
         s: pltpu.make_async_copy(branch_ref.at[:, :, :, column(s)], branch[s], branch_sem.at[s]) for s in sequence}
@@ -97,8 +119,11 @@
         where = () if h is None else (slice(None), slice(None), halves[h])
         return pltpu.make_async_remote_copy(
             src_ref=sent.at[(s, j, *where)], dst_ref=got.at[(s, q, *where)], send_sem=send_sem.at[s],
-            recv_sem=recv_sem.at[s] if h is None else last_sem.at[h],
+            recv_sem=last_sem.at[h] if s == last else recv_sem.at[s],
             device_id={"mode": flip(z, s, groups) * per + j}, device_id_type=MESH)
+
+    def await_bytes(place, sem):
+        pltpu.make_async_copy(place, place, sem).wait()
 
     def own(s):
         return pltpu.make_async_copy(sent.at[s, q], got.at[s, q], recv_sem.at[s])
@@ -112,35 +137,47 @@
                 own(s).start() if s == 0 and i == 0 else hop(s, i, h).start()
 
     highs, lows = [], []
-    parcels = [range(HEAD), range(HEAD, per)]
-    cut = 2 * HEAD * rows
+    parcels = [range(per // 2), range(per // 2, per)]
     by = [None, None]
 
-    def send_lead(by, which):
+    def send_lead(by, which, h=None):
         m = by[0].shape[0] // 2
-        send(lead, by[0][:m] - by[1][m:], by[1][:m] + by[0][m:], which)
-
-    for h, half in enumerate(halves):
-        left_copies[h].wait()
+        side = slice(None) if h is None else slice(h * (bw // 2), (h + 1) * (bw // 2))
+        for part, value in enumerate((by[0][:m] - by[1][m:], by[1][:m] + by[0][m:])):
+            for place, j in enumerate(which):
+                sent[lead, j, part, :, side] = value[place * rows:(place + 1) * rows]
+        for j in which:
+            hop(lead, j, h).start()
+
+    left_side, right_side = slice(0, bw // 2), slice(bw // 2, bw)
+    for k, half in enumerate(halves):
+        left_copies[k].wait()
         high, low = split(jnp.concatenate([
-            left[h][o0, part].T[which[0] * rows:(which[-1] + 1) * rows] for which in parcels for part in range(2)], axis=0))
+            left[k][o0, part].T[which[0] * rows:(which[-1] + 1) * rows] for which in parcels for part in range(2)], axis=0))
         highs.append(high)
         lows.append(low)
+        stem_copies[k].wait()
         for part in range(2):
-            stem_copies[h][part].wait()
-            if h == part == 1:
-                for s in sequence[1:] + [lead]:
-                    branch_copies[s].start()
-            xh[part, half], xl[part, half] = split(stem[part, half])
-            both_parts = dot(jnp.concatenate([high[:cut], low[:cut]], axis=0), xh[part, half])
-            add = both_parts[:cut] + (both_parts[cut:] + dot(high[:cut], xl[part, half]))
-            by[part] = add if h == 0 else by[part] + add
-    pl.semaphore_wait(barrier, n - 1)
-    send_lead(by, parcels[0])
-    high, low = (jnp.concatenate([piece[cut:] for piece in pieces], axis=1) for pieces in (highs, lows))
-    send_lead([dot3(high, low, xh[part], xl[part]) for part in range(2)], parcels[1])
+            xh[part, half, left_side], xl[part, half, left_side] = split(stem[part, half, left_side])
+            add = dot3(high[:LANES], low[:LANES], xh[part, half, left_side], xl[part, half, left_side])
+            by[part] = add if k == 0 else by[part] + add
+    enter()
+    send_lead(by, parcels[0], 0)
+    side_copy.wait()
+    for s in sequence[1:] + [lead]:
+        branch_copies[s].start()
+    for part in range(2):
+        xh[part, :, right_side], xl[part, :, right_side] = split(stem[part, :, right_side])
+    high, low = (jnp.concatenate([piece[:LANES] for piece in pieces], axis=1) for pieces in (highs, lows))
+    send_lead([dot3(high, low, xh[part, :, right_side], xl[part, :, right_side]) for part in range(2)], parcels[0], 1)
+    high, low = (jnp.concatenate([piece[LANES:] for piece in pieces], axis=1) for pieces in (highs, lows))
+    rest = [dot3(high, low, xh[part], xl[part]) for part in range(2)]
+    pl.when(z == middle - 1)(lambda: pl.semaphore_wait(notice_top, per // 2))
+    send_lead(rest, parcels[1])
     for s in early[1:]:
         branch_copies[s].wait()
+        if s == near:
+            pl.when(z == middle)(lambda: pl.semaphore_wait(notice_low, per))
         send(s, *first_rows(s))
     for s in sequence[len(early):] + [lead]:
         branch_copies[s].wait()
@@ -180,9 +217,6 @@
 
     arrivals = [0] + [s for s in early if s != groups // 2] + [groups // 2] + [s for s in sequence[len(early):] if s]
     tile = 2 * LANES
-
-    def await_bytes(place, sem):
-        pltpu.make_async_copy(place, place, sem).wait()
 
     def arrived(s, side):
         return jnp.concatenate([got[s, j, part, :, side] for part in range(2) for j in range(per)], axis=0)
@@ -257,12 +291,15 @@
             pltpu.VMEM((groups, per, 2, rows, bw), F32),
             pltpu.SMEM(branch_order.shape, jnp.int32),
             pltpu.SemaphoreType.DMA,
-            pltpu.SemaphoreType.DMA((2, 2)),
+            pltpu.SemaphoreType.DMA((2,)),
             pltpu.SemaphoreType.DMA((2,)),
             pltpu.SemaphoreType.DMA((groups,)),
             pltpu.SemaphoreType.DMA((groups,)),
             pltpu.SemaphoreType.DMA((groups,)),
             pltpu.SemaphoreType.DMA((2,)),
+            pltpu.SemaphoreType.DMA,
+            pltpu.SemaphoreType.REGULAR,
+            pltpu.SemaphoreType.REGULAR,
             *[pltpu.VMEM((4, 2, bw // 2, LANES), F32)] * 2,
             *[pltpu.VMEM((4, 2, bw, LANES), F32)] * groups,
         ],

time: 51.9 us -> 51.4 us (level)
  no operation moved by 1% of the time
where the time goes in v4:
time: 51.4 us; the launch traced here: 51.3 us
  Pallas kernels  51.3 us (100%)
    pallas_call x1, Pallas kernels, fused(): pl.pallas_call(functools.partial(kernel, n), out_shape=[jax.ShapeDtypeStr...  49.9 us
    pallas_call x1, Pallas kernels, fused(): pl.pallas_call(finish, out_shape=jax.ShapeDtypeStruct((2, bw, bw), F32),...  1.4 us

profile of v4, /device:TPU:8, one launch (start us, length us, event | category | flops | bytes accessed | tf_op | source)
XLA Modules:
  0.0 51.3 jit_solution(1518491170485907567)
XLA Ops:
  0.0 49.9 %shard_map.37 = (f32[2,512,512]{2,1,0:T(8,128)S(1)}, bf16[1024,256]{1,0:T(8,128)(2,1)S(1)}, bf16[1024,256]{1,0:T(8,128)(2,1)S(1)}, bf16[256,256]{1,0:T(8,128)(2,1)S(1)}, bf16[256,256]{1,0:T(8,128)(2,1)S(1)}) custom-call(s32[4]{0:T(128)} %order_ref.1, f32[2,512,512]{2,1,0:T(8,128)} %bitcast.4, f32[4,2,512,512]{3,2,1,0:T(8,128)} %branch_ref.1), custom_call_target="tpu_custom_call" | custom-call | tf_op jit(solution)/shard_map/pallas_call | solution.py:276
  49.9 1.4 %shard_map.38 = f32[2,512,512]{2,1,0:T(8,128)} custom-call(f32[2,512,512]{2,1,0:T(8,128)S(1)} %get-tuple-element.10.acc_ref, bf16[1024,256]{1,0:T(8,128)(2,1)S(1)} %get-tuple-element.11.high_ref, bf16[1024,256]{1,0:T(8,128)(2,1)S(1)} %get-tuple-element.12.low_ref, bf16[256,256]{1,0:T(8,128)(2,1)S(1)} %get-tuple-element.13.right_high, ...), custom_call_target="tpu_custom_call" | custom-call | tf_op jit(solution)/shard_map/pallas_call | solution.py:308

commit v5 on v4

--- a/solution.py
+++ b/solution.py
@@ -43,7 +43,7 @@
 
 
 def kernel(n, order_ref, stem_ref, branch_ref, out_ref, last_high, last_low, tail_high, tail_low, stem, xh, xl, bh, bl, dh, dl, wh, wl,
-           lch, lcl, sent, got, order, order_sem, stem_sem, left_sem, branch_sem, send_sem, recv_sem, last_sem, side_sem, notice_low, notice_top, left_0, left_1, *branch):
+           lch, lcl, sent, got, order, order_sem, stem_sem, left_sem, side_sem, send_sem, recv_sem, notice, left_0, left_1, *branch):
     bw = stem.shape[1]
     rows = bw // n
     per = LANES // rows
@@ -57,32 +57,6 @@
 
     def column(s):
         return pl.ds(pl.multiple_of(flip(z, s, groups) * LANES, LANES), LANES)
-
-    barrier = pltpu.get_barrier_semaphore()
-    top, middle = groups - 1, groups // 2
-    near = middle ^ top
-
-    def greet(sem, s, k):
-        pl.semaphore_signal(
-            sem, inc=1, device_id={"mode": flip(z, s, groups) * per + flip(q, k, per)}, device_id_type=MESH)
-
-    for s in range(groups - 1, -1, -1):
-        for k in range(per):
-            if s == near:
-                pl.when(z != top)(functools.partial(greet, barrier, s, k))
-            elif s == lead:
-                pl.when(z + upper != top + 1)(functools.partial(greet, barrier, s, k))
-            elif s or k:
-                greet(barrier, s, k)
-
-    def equal(a, b):
-        return (a == b).astype(jnp.int32)
-
-    def enter():
-        pl.semaphore_wait(barrier, n - 1 - per * equal(z, middle) - per // 2 * equal(z, middle - 1))
-        for k in range(per):
-            pl.when(z == top)(functools.partial(greet, notice_low, near, k))
-            pl.when(z + upper == top + 1)(functools.partial(greet, notice_top, lead, k))
 
     order_copy = pltpu.make_async_copy(order_ref, order, order_sem)
     order_copy.start()
@@ -95,8 +69,36 @@
     side_copy = pltpu.make_async_copy(stem_ref.at[:, :, halves[1]], stem.at[:, :, halves[1]], side_sem)
     for copy in (left_copies[0], stem_copies[0], left_copies[1], stem_copies[1], side_copy):
         copy.start()
+    barrier = pltpu.get_barrier_semaphore()
+    top, middle = groups - 1, groups // 2
+    near = middle ^ top
+
+    def greet(sem, s, k):
+        pl.semaphore_signal(
+            sem, inc=1, device_id={"mode": flip(z, s, groups) * per + flip(q, k, per)}, device_id_type=MESH)
+
+    for s in range(groups - 1, -1, -1):
+        for k in range(per):
+            if s == near:
+                pl.when(z != top)(functools.partial(greet, barrier, s, k))
+            elif s == lead:
+                pl.when(z + upper != top + 1)(functools.partial(greet, barrier, s, k))
+            elif s or k:
+                greet(barrier, s, k)
+
+    def equal(a, b):
+        return (a == b).astype(jnp.int32)
+
+    def enter():
+        pl.semaphore_wait(barrier, n - 1 - per * equal(z, middle) - per // 2 * equal(z, middle - 1))
+        for k in range(per):
+            pl.when(z == top)(functools.partial(greet, notice, near, k))
+            pl.when(z + upper == top + 1)(functools.partial(greet, notice, lead, k))
+
+    free = [left_sem.at[0], stem_sem.at[0], left_sem.at[1], stem_sem.at[1]]
     branch_copies = {
-        s: pltpu.make_async_copy(branch_ref.at[:, :, :, column(s)], branch[s], branch_sem.at[s]) for s in sequence}
+        s: pltpu.make_async_copy(branch_ref.at[:, :, :, column(s)], branch[s], sem)
+        for s, sem in zip(sequence[1:] + [lead], free)}
     order_copy.wait()
     o0, o1, o2, o3 = (order[k] for k in range(4))
 
@@ -118,20 +120,20 @@
         j = partner(s, i)
         where = () if h is None else (slice(None), slice(None), halves[h])
         return pltpu.make_async_remote_copy(
-            src_ref=sent.at[(s, j, *where)], dst_ref=got.at[(s, q, *where)], send_sem=send_sem.at[s],
-            recv_sem=last_sem.at[h] if s == last else recv_sem.at[s],
+            src_ref=sent.at[(s * per + j, *where)], dst_ref=got.at[(s, q, *where)], send_sem=send_sem,
+            recv_sem=recv_sem.at[groups - 1 + h if s == last else s - (s > last)],
             device_id={"mode": flip(z, s, groups) * per + j}, device_id_type=MESH)
 
     def await_bytes(place, sem):
         pltpu.make_async_copy(place, place, sem).wait()
 
     def own(s):
-        return pltpu.make_async_copy(sent.at[s, q], got.at[s, q], recv_sem.at[s])
+        return pltpu.make_async_copy(sent.at[s * per + q], got.at[s, q], recv_sem.at[s - (s > last)])
 
     def send(s, real, imag, which=range(per)):
         for place, j in enumerate(which):
-            sent[s, j, 0] = real[place * rows:(place + 1) * rows]
-            sent[s, j, 1] = imag[place * rows:(place + 1) * rows]
+            sent[s * per + j, 0] = real[place * rows:(place + 1) * rows]
+            sent[s * per + j, 1] = imag[place * rows:(place + 1) * rows]
         for h in range(2) if s == last else [None]:
             for i in which:
                 own(s).start() if s == 0 and i == 0 else hop(s, i, h).start()
@@ -145,7 +147,7 @@
         side = slice(None) if h is None else slice(h * (bw // 2), (h + 1) * (bw // 2))
         for part, value in enumerate((by[0][:m] - by[1][m:], by[1][:m] + by[0][m:])):
             for place, j in enumerate(which):
-                sent[lead, j, part, :, side] = value[place * rows:(place + 1) * rows]
+                sent[lead * per + j, part, :, side] = value[place * rows:(place + 1) * rows]
         for j in which:
             hop(lead, j, h).start()
 
@@ -172,12 +174,12 @@
     send_lead([dot3(high, low, xh[part, :, right_side], xl[part, :, right_side]) for part in range(2)], parcels[0], 1)
     high, low = (jnp.concatenate([piece[LANES:] for piece in pieces], axis=1) for pieces in (highs, lows))
     rest = [dot3(high, low, xh[part], xl[part]) for part in range(2)]
-    pl.when(z == middle - 1)(lambda: pl.semaphore_wait(notice_top, per // 2))
+    pl.when(z == middle - 1)(lambda: pl.semaphore_wait(notice, per // 2))
     send_lead(rest, parcels[1])
     for s in early[1:]:
         branch_copies[s].wait()
         if s == near:
-            pl.when(z == middle)(lambda: pl.semaphore_wait(notice_low, per))
+            pl.when(z == middle)(lambda: pl.semaphore_wait(notice, per))
         send(s, *first_rows(s))
     for s in sequence[len(early):] + [lead]:
         branch_copies[s].wait()
@@ -223,10 +225,10 @@
 
     for index, s in enumerate(arrivals):
         if s == last:
-            await_bytes(got.at[last, :, :, :, halves[0]], last_sem.at[0])
+            await_bytes(got.at[last, :, :, :, halves[0]], recv_sem.at[groups - 1])
             side = slice(0, bw // 2)
         else:
-            await_bytes(got.at[s], recv_sem.at[s])
+            await_bytes(got.at[s], recv_sem.at[s - (s > last)])
             side = slice(0, bw)
         right = arrived(s, side)
         if s in early:
@@ -239,28 +241,23 @@
             place = (part, slice(row, row + tile), side)
             add = dot3(high_ref[at], low_ref[at], right_high, right_low)
             out_ref[place] = add if index == 0 else out_ref[place] + add
-    for s in range(groups):
-        await_bytes(sent.at[s, pl.ds(0, per if s else per - 1)], send_sem.at[s])
-    await_bytes(got.at[last, :, :, :, halves[1]], last_sem.at[1])
+    await_bytes(sent.at[pl.ds(0, n - 1)], send_sem)
+    await_bytes(got.at[last, :, :, :, halves[1]], recv_sem.at[groups])
     tail_high[...], tail_low[...] = split(arrived(last, slice(bw // 2, bw)))
 
 
-def finish(acc_ref, high_ref, low_ref, right_high, right_low, out_ref, tiles, side_sem, sem):
+def finish(acc_ref, high_ref, low_ref, right_high, right_low, out_ref, tiles, sem):
     count, tile, half = tiles.shape
-    copies = []
-    for part in range(2):
-        at = (part, slice(None), pl.ds(0, half))
-        copies.append(pltpu.make_async_copy(acc_ref.at[at], out_ref.at[at], side_sem.at[part]))
-        copies[part].start()
+    ready = pltpu.make_async_copy(acc_ref.at[:, :, pl.ds(0, half)], out_ref.at[:, :, pl.ds(0, half)], sem.at[0])
+    ready.start()
     right = right_high[...], right_low[...]
     for i in range(count):
         part, row = divmod(i * tile, 2 * half)
         at = slice(i * tile, (i + 1) * tile)
         tiles[i] = acc_ref[part, row:row + tile, half:] + dot3(high_ref[at], low_ref[at], *right)
-        copies.append(pltpu.make_async_copy(tiles.at[i], out_ref.at[part, pl.ds(row, tile), pl.ds(half, half)], sem.at[i]))
-        copies[-1].start()
-    for copy in copies:
-        copy.wait()
+        pltpu.make_async_copy(tiles.at[i], out_ref.at[part, pl.ds(row, tile), pl.ds(half, half)], sem.at[1]).start()
+    ready.wait()
+    pltpu.make_async_copy(tiles, tiles, sem.at[1]).wait()
 
 
 def fused(n, stem_tensor, branch_tensors, branch_order):
@@ -287,18 +284,15 @@
             *[square] * 8,
             window,
             window,
-            pltpu.VMEM((groups, per, 2, rows, bw), F32),
+            pltpu.VMEM((n, 2, rows, bw), F32),
             pltpu.VMEM((groups, per, 2, rows, bw), F32),
             pltpu.SMEM(branch_order.shape, jnp.int32),
             pltpu.SemaphoreType.DMA,
             pltpu.SemaphoreType.DMA((2,)),
             pltpu.SemaphoreType.DMA((2,)),
-            pltpu.SemaphoreType.DMA((groups,)),
-            pltpu.SemaphoreType.DMA((groups,)),
-            pltpu.SemaphoreType.DMA((groups,)),
-            pltpu.SemaphoreType.DMA((2,)),
             pltpu.SemaphoreType.DMA,
-            pltpu.SemaphoreType.REGULAR,
+            pltpu.SemaphoreType.DMA,
+            pltpu.SemaphoreType.DMA((groups + 1,)),
             pltpu.SemaphoreType.REGULAR,
             *[pltpu.VMEM((4, 2, bw // 2, LANES), F32)] * 2,
             *[pltpu.VMEM((4, 2, bw, LANES), F32)] * groups,
@@ -310,7 +304,7 @@
         out_shape=jax.ShapeDtypeStruct((2, bw, bw), F32),
         in_specs=[vmem] * 5,
         out_specs=pl.BlockSpec(memory_space=pl.ANY),
-        scratch_shapes=[pltpu.VMEM((tiles, LANES, bw // 2), F32), pltpu.SemaphoreType.DMA((2,)), pltpu.SemaphoreType.DMA((tiles,))],
+        scratch_shapes=[pltpu.VMEM((tiles, LANES, bw // 2), F32), pltpu.SemaphoreType.DMA((2,))],
         compiler_params=pltpu.CompilerParams(vmem_limit_bytes=8 << 20),
     )(*partial).reshape(stem_tensor.shape)
 

time: 51.4 us -> 51.2 us (level)
  no operation moved by 1% of the time
where the time goes in v5:
time: 51.2 us; the launch traced here: 51.1 us
  Pallas kernels  51.1 us (100%)
    pallas_call x1, Pallas kernels, fused(): pl.pallas_call(functools.partial(kernel, n), out_shape=[jax.ShapeDtypeStr...  49.7 us
    pallas_call x1, Pallas kernels, fused(): pl.pallas_call(finish, out_shape=jax.ShapeDtypeStruct((2, bw, bw), F32),...  1.33 us

profile of v5, /device:TPU:8, one launch (start us, length us, event | category | flops | bytes accessed | tf_op | source)
XLA Modules:
  0.0 51.1 jit_solution(5177479842135742878)
XLA Ops:
  0.0 49.7 %shard_map.37 = (f32[2,512,512]{2,1,0:T(8,128)S(1)}, bf16[1024,256]{1,0:T(8,128)(2,1)S(1)}, bf16[1024,256]{1,0:T(8,128)(2,1)S(1)}, bf16[256,256]{1,0:T(8,128)(2,1)S(1)}, bf16[256,256]{1,0:T(8,128)(2,1)S(1)}) custom-call(s32[4]{0:T(128)} %order_ref.1, f32[2,512,512]{2,1,0:T(8,128)} %bitcast.4, f32[4,2,512,512]{3,2,1,0:T(8,128)} %branch_ref.1), custom_call_target="tpu_custom_call" | custom-call | tf_op jit(solution)/shard_map/pallas_call | solution.py:273
  49.7 1.3 %shard_map.38 = f32[2,512,512]{2,1,0:T(8,128)} custom-call(f32[2,512,512]{2,1,0:T(8,128)S(1)} %get-tuple-element.10.acc_ref, bf16[1024,256]{1,0:T(8,128)(2,1)S(1)} %get-tuple-element.11.high_ref, bf16[1024,256]{1,0:T(8,128)(2,1)S(1)} %get-tuple-element.12.low_ref, bf16[256,256]{1,0:T(8,128)(2,1)S(1)} %get-tuple-element.13.right_high, ...), custom_call_target="tpu_custom_call" | custom-call | tf_op jit(solution)/shard_map/pallas_call | solution.py:302

commit v6 on v5

--- a/solution.py
+++ b/solution.py
@@ -91,6 +91,8 @@
 
     def enter():
         pl.semaphore_wait(barrier, n - 1 - per * equal(z, middle) - per // 2 * equal(z, middle - 1))
+
+    def announce():
         for k in range(per):
             pl.when(z == top)(functools.partial(greet, notice, near, k))
             pl.when(z + upper == top + 1)(functools.partial(greet, notice, lead, k))
@@ -165,6 +167,7 @@
             by[part] = add if k == 0 else by[part] + add
     enter()
     send_lead(by, parcels[0], 0)
+    announce()
     side_copy.wait()
     for s in sequence[1:] + [lead]:
         branch_copies[s].start()

time: 51.2 us -> 51.2 us (level)
  no operation moved by 1% of the time
where the time goes in v6:
time: 51.2 us; the launch traced here: 51.1 us
  Pallas kernels  51 us (100%)
    pallas_call x1, Pallas kernels, fused(): pl.pallas_call(functools.partial(kernel, n), out_shape=[jax.ShapeDtypeStr...  49.7 us
    pallas_call x1, Pallas kernels, fused(): pl.pallas_call(finish, out_shape=jax.ShapeDtypeStruct((2, bw, bw), F32),...  1.33 us

profile of v6, /device:TPU:8, one launch (start us, length us, event | category | flops | bytes accessed | tf_op | source)
XLA Modules:
  0.0 51.1 jit_solution(2281662410076317347)
XLA Ops:
  0.0 49.7 %shard_map.37 = (f32[2,512,512]{2,1,0:T(8,128)S(1)}, bf16[1024,256]{1,0:T(8,128)(2,1)S(1)}, bf16[1024,256]{1,0:T(8,128)(2,1)S(1)}, bf16[256,256]{1,0:T(8,128)(2,1)S(1)}, bf16[256,256]{1,0:T(8,128)(2,1)S(1)}) custom-call(s32[4]{0:T(128)} %order_ref.1, f32[2,512,512]{2,1,0:T(8,128)} %bitcast.4, f32[4,2,512,512]{3,2,1,0:T(8,128)} %branch_ref.1), custom_call_target="tpu_custom_call" | custom-call | tf_op jit(solution)/shard_map/pallas_call | solution.py:276
  49.7 1.3 %shard_map.38 = f32[2,512,512]{2,1,0:T(8,128)} custom-call(f32[2,512,512]{2,1,0:T(8,128)S(1)} %get-tuple-element.10.acc_ref, bf16[1024,256]{1,0:T(8,128)(2,1)S(1)} %get-tuple-element.11.high_ref, bf16[1024,256]{1,0:T(8,128)(2,1)S(1)} %get-tuple-element.12.low_ref, bf16[256,256]{1,0:T(8,128)(2,1)S(1)} %get-tuple-element.13.right_high, ...), custom_call_target="tpu_custom_call" | custom-call | tf_op jit(solution)/shard_map/pallas_call | solution.py:305

commit v7 on v5

--- a/solution.py
+++ b/solution.py
@@ -61,6 +61,7 @@
     order_copy = pltpu.make_async_copy(order_ref, order, order_sem)
     order_copy.start()
     halves = [pl.ds(h * (bw // 2), bw // 2) for h in range(2)]
+    ends = [pl.ds(0, bw - LANES), pl.ds(bw - LANES, LANES)]
     left = (left_0, left_1)
     left_copies = [pltpu.make_async_copy(
         branch_ref.at[:, :, half, column(lead)], left[h], left_sem.at[h]) for h, half in enumerate(halves)]
@@ -118,7 +119,7 @@
 
     def hop(s, i, h=None):
         j = partner(s, i)
-        where = () if h is None else (slice(None), slice(None), halves[h])
+        where = () if h is None else (slice(None), slice(None), (ends if s == last else halves)[h])
         return pltpu.make_async_remote_copy(
             src_ref=sent.at[(s * per + j, *where)], dst_ref=got.at[(s, q, *where)], send_sem=send_sem,
             recv_sem=recv_sem.at[groups - 1 + h if s == last else s - (s > last)],
@@ -225,8 +226,8 @@
 
     for index, s in enumerate(arrivals):
         if s == last:
-            await_bytes(got.at[last, :, :, :, halves[0]], recv_sem.at[groups - 1])
-            side = slice(0, bw // 2)
+            await_bytes(got.at[last, :, :, :, ends[0]], recv_sem.at[groups - 1])
+            side = slice(0, bw - LANES)
         else:
             await_bytes(got.at[s], recv_sem.at[s - (s > last)])
             side = slice(0, bw)
@@ -242,20 +243,22 @@
             add = dot3(high_ref[at], low_ref[at], right_high, right_low)
             out_ref[place] = add if index == 0 else out_ref[place] + add
     await_bytes(sent.at[pl.ds(0, n - 1)], send_sem)
-    await_bytes(got.at[last, :, :, :, halves[1]], recv_sem.at[groups])
-    tail_high[...], tail_low[...] = split(arrived(last, slice(bw // 2, bw)))
+    await_bytes(got.at[last, :, :, :, ends[1]], recv_sem.at[groups])
+    tail_high[...], tail_low[...] = split(arrived(last, slice(bw - LANES, bw)))
 
 
 def finish(acc_ref, high_ref, low_ref, right_high, right_low, out_ref, tiles, sem):
-    count, tile, half = tiles.shape
-    ready = pltpu.make_async_copy(acc_ref.at[:, :, pl.ds(0, half)], out_ref.at[:, :, pl.ds(0, half)], sem.at[0])
+    count, tile, width = tiles.shape
+    bw = acc_ref.shape[-1]
+    begin = bw - width
+    ready = pltpu.make_async_copy(acc_ref.at[:, :, pl.ds(0, begin)], out_ref.at[:, :, pl.ds(0, begin)], sem.at[0])
     ready.start()
     right = right_high[...], right_low[...]
     for i in range(count):
-        part, row = divmod(i * tile, 2 * half)
+        part, row = divmod(i * tile, bw)
         at = slice(i * tile, (i + 1) * tile)
-        tiles[i] = acc_ref[part, row:row + tile, half:] + dot3(high_ref[at], low_ref[at], *right)
-        pltpu.make_async_copy(tiles.at[i], out_ref.at[part, pl.ds(row, tile), pl.ds(half, half)], sem.at[1]).start()
+        tiles[i] = acc_ref[part, row:row + tile, begin:] + dot3(high_ref[at], low_ref[at], *right)
+        pltpu.make_async_copy(tiles.at[i], out_ref.at[part, pl.ds(row, tile), pl.ds(begin, width)], sem.at[1]).start()
     ready.wait()
     pltpu.make_async_copy(tiles, tiles, sem.at[1]).wait()
 
@@ -269,13 +272,13 @@
     hbm = functools.partial(pltpu.with_memory_space_constraint, memory_space=pltpu.HBM)
     window = pltpu.VMEM((groups, 2 * bw, 2 * LANES), BF16)
     vmem = pl.BlockSpec(memory_space=pltpu.VMEM)
-    tiles = 2 * bw // LANES
+    tiles = bw // LANES
     partial = pl.pallas_call(
         functools.partial(kernel, n),
         out_shape=[
             jax.ShapeDtypeStruct((2, bw, bw), F32),
             *[jax.ShapeDtypeStruct((2 * bw, 2 * LANES), BF16)] * 2,
-            *[jax.ShapeDtypeStruct((2 * LANES, bw // 2), BF16)] * 2,
+            *[jax.ShapeDtypeStruct((2 * LANES, LANES), BF16)] * 2,
         ],
         in_specs=[pl.BlockSpec(memory_space=pl.ANY)] * 3,
         out_specs=[vmem] * 5,
@@ -304,7 +307,7 @@
         out_shape=jax.ShapeDtypeStruct((2, bw, bw), F32),
         in_specs=[vmem] * 5,
         out_specs=pl.BlockSpec(memory_space=pl.ANY),
-        scratch_shapes=[pltpu.VMEM((tiles, LANES, bw // 2), F32), pltpu.SemaphoreType.DMA((2,))],
+        scratch_shapes=[pltpu.VMEM((tiles, 2 * LANES, LANES), F32), pltpu.SemaphoreType.DMA((2,))],
         compiler_params=pltpu.CompilerParams(vmem_limit_bytes=8 << 20),
     )(*partial).reshape(stem_tensor.shape)
 

time: 51.2 us -> 51.5 us (level)
  no operation moved by 1% of the time
where the time goes in v7:
time: 51.5 us; the launch traced here: 51.3 us
  Pallas kernels  51.3 us (100%)
    pallas_call x1, Pallas kernels, fused(): pl.pallas_call(functools.partial(kernel, n), out_shape=[jax.ShapeDtypeStr...  50 us
    pallas_call x1, Pallas kernels, fused(): pl.pallas_call(finish, out_shape=jax.ShapeDtypeStruct((2, bw, bw), F32),...  1.33 us

profile of v7, /device:TPU:8, one launch (start us, length us, event | category | flops | bytes accessed | tf_op | source)
XLA Modules:
  0.0 51.3 jit_solution(7036737899550808259)
XLA Ops:
  0.0 50.0 %shard_map.37 = (f32[2,512,512]{2,1,0:T(8,128)S(1)}, bf16[1024,256]{1,0:T(8,128)(2,1)S(1)}, bf16[1024,256]{1,0:T(8,128)(2,1)S(1)}, bf16[256,128]{1,0:T(8,128)(2,1)S(1)}, bf16[256,128]{1,0:T(8,128)(2,1)S(1)}) custom-call(s32[4]{0:T(128)} %order_ref.1, f32[2,512,512]{2,1,0:T(8,128)} %bitcast.4, f32[4,2,512,512]{3,2,1,0:T(8,128)} %branch_ref.1), custom_call_target="tpu_custom_call" | custom-call | tf_op jit(solution)/shard_map/pallas_call | solution.py:276
  50.0 1.3 %shard_map.38 = f32[2,512,512]{2,1,0:T(8,128)} custom-call(f32[2,512,512]{2,1,0:T(8,128)S(1)} %get-tuple-element.10.acc_ref, bf16[1024,256]{1,0:T(8,128)(2,1)S(1)} %get-tuple-element.11.high_ref, bf16[1024,256]{1,0:T(8,128)(2,1)S(1)} %get-tuple-element.12.low_ref, bf16[256,128]{1,0:T(8,128)(2,1)S(1)} %get-tuple-element.13.right_high, ...), custom_call_target="tpu_custom_call" | custom-call | tf_op jit(solution)/shard_map/pallas_call | solution.py:305
